TPU v7x, 32 devices: a whole 2x2x4 slice. The times are simulated.
32 devices in a mesh: tm: 8 (over z, core), space: 4 (over y, x).
Axes of the slice: x: 2, y: 2, z: 4, core: 2. Of those that a mesh axis runs over, the one named last changes fastest.
Arguments:
- snapshots: bfloat16 [4096, 12288], P('tm', 'space')
- freq_ids: int32 [64], replicated, may hold values from 0 to 127
Outputs:
- gram: float32 [64, 2, 15, 15], P('tm')
All inputs are finite; a program needn't handle non-finite values.
Results may differ from a plain program's by a relative error of at most 0.00039.
Values may be sent and summed in bfloat16 or wider, within the bound.
No kernel may reach another device: no remote copies, remote signals or barrier semaphores. Data moves between devices by JAX's collectives and lax.ppermute only.
A program may use at most 64 MiB of HBM per device.

v0:
```python
import math

import jax
import jax.numpy as jnp
from jax import lax
from jax.sharding import PartitionSpec as P

NFFT = 512
F = 64


def shifted(block, axis, distance):
    devices = range(lax.axis_size(axis))
    route = [(i - distance, i) for i in devices if i - distance in devices]
    return lax.ppermute(block, axis, route)


def kernel_values(freqs, shifts, window_length):
    phase = freqs * shifts % window_length
    angle = 2.0 * math.pi / window_length * phase.astype(jnp.float32)
    window = 0.5 - 0.5 * jnp.cos(2.0 * math.pi / window_length * shifts.astype(jnp.float32))
    return (window * jnp.cos(angle), -window * jnp.sin(angle))


def local(snapshots, freq_ids):
    hop_len = NFFT // 2
    count_tm = lax.axis_size("tm")
    blocks = 2 * count_tm - 1
    device = lax.axis_index("tm")
    points = snapshots.shape[1]
    shifts = jnp.arange(NFFT, dtype=jnp.int32)
    real_part, imag_part = kernel_values(freq_ids[:, None], shifts[None, :], NFFT)
    table = jnp.stack([real_part, imag_part], axis=1).reshape(2 * F, NFFT).astype(jnp.bfloat16)
    leading = shifted(snapshots[:hop_len], "tm", -1)
    extended = jnp.concatenate([snapshots, leading], axis=0)
    pieces = []
    for slot in range(2):
        block = device * 2 + slot
        segment = extended[hop_len * slot : hop_len * slot + NFFT]
        result = jnp.dot(table, segment, preferred_element_type=jnp.float32)
        pieces.append(jnp.where(block < blocks, result, 0.0))
    owned = jnp.stack(pieces, axis=0).astype(jnp.bfloat16)
    owned = owned.reshape(2, F, 2, points)
    by_freq = lax.all_to_all(owned, "tm", split_axis=1, concat_axis=0, tiled=True)
    slots_all = by_freq.shape[0]
    resident_frequencies = by_freq.shape[1]
    stacked_snapshot_rows = jnp.transpose(by_freq, (1, 2, 0, 3)).reshape(
        resident_frequencies, 2 * slots_all, points
    )
    cross_product_terms = jnp.einsum(
        "tnf,tof->tno",
        stacked_snapshot_rows,
        stacked_snapshot_rows,
        preferred_element_type=jnp.float32,
    )
    gram_real_matrix = (
        cross_product_terms[:, :slots_all, :slots_all]
        + cross_product_terms[:, slots_all:, slots_all:]
    )
    imag_gram = (
        cross_product_terms[:, slots_all:, :slots_all]
        - cross_product_terms[:, :slots_all, slots_all:]
    )
    scale = 1.0 / (NFFT * points * lax.axis_size("space"))
    resident_gram_matrix = (
        jnp.stack([gram_real_matrix, imag_gram], axis=1)[:, :, :blocks, :blocks] * scale
    )
    return lax.psum(resident_gram_matrix, "space")


def solution(mesh):
    return jax.shard_map(
        local,
        mesh=mesh,
        in_specs=(P("tm", "space"), P()),
        out_specs=P("tm", None, None, None),
        check_vma=False,
    )
```

profile of v0, /device:TPU:0, one launch (start us, length us, event | category | flops | bytes accessed | tf_op | source)
XLA Modules:
  0.0 96.8 jit_solution(8468911311742353693)
XLA Ops:
  0.0 0.0 copy-start
  0.0 0.0 copy-start.2
  0.0 2.8 %slice.21 = bf16[256,3072]{1,0:T(8,128)(2,1)} slice(bf16[512,3072]{1,0:T(8,128)(2,1)} %param.2), slice={[0:256], [0:3072]} | slice | bytes 3145728 | tf_op jit(solution)/shard_map/slice | solution.py:34
  2.8 1.3 %collective-permute-start = (bf16[256,3072]{1,0:T(8,128)(2,1)}, bf16[256,3072]{1,0:T(8,128)(2,1)}, u32[]{:S(2)}, u32[]{:S(2)}) collective-permute-start(bf16[256,3072]{1,0:T(8,128)(2,1)} %slice.21), channel_id=1, source_target_pairs={{4,0},{8,4},{12,8},{16,12},{20,16},{24,20},{28,24},{5,1},{9,5},{13... | collective-permute-start | bytes 4718600 | tf_op jit(solution)/shard_map/ppermute | solution.py:15
  4.2 0.0 copy-done.2
  4.2 0.6 multiply_convert_fusion.1
  4.8 0.1 copy.13
  5.0 0.1 convert_element_type.35
  5.0 0.0 copy-done
  5.0 1.5 %fusion = bf16[128,3072]{1,0:T(8,128)(2,1)} fusion(bf16[128,512]{1,0:T(8,128)(2,1)S(1)} %convert_element_type.35, bf16[512,3072]{1,0:T(8,128)(2,1)S(1)} %copy-done, pred[]{:T(512)S(6)} %lt.12), kind=kOutput, calls=%fused_computation.2 | convolution fusion | flops 403439616 | bytes 4063233 | tf_op jit(solution)/shard_map/dot_general | solution.py:40
  6.5 2.8 %stack.25 = bf16[1,64,2,3072]{3,2,1,0:T(2,128)(2,1)} reshape(bf16[128,3072]{1,0:T(8,128)(2,1)} %fusion) | data formatting | bytes 1572864 | tf_op jit(solution)/shard_map/stack | solution.py:42
  9.4 0.0 collective-permute-done
  9.4 2.9 %fusion.1 = bf16[128,3072]{1,0:T(8,128)(2,1)} fusion(bf16[128,512]{1,0:T(8,128)(2,1)S(1)} %convert_element_type.35, bf16[256,3072]{1,0:T(8,128)(2,1)} %collective-permute-done, bf16[512,3072]{1,0:T(8,128)(2,1)S(1)} %copy-done, pred[]{:T(512)S(6)} %lt.14), kind=kOutput, calls=%fused_computation.3 | convolution fusion | flops 409731072 | bytes 5636097 | tf_op jit(solution)/shard_map/dot_general | solution.py:40
  12.3 0.0 copy-start.1
  12.3 2.2 %stack.26 = bf16[1,64,2,3072]{3,2,1,0:T(2,128)(2,1)S(1)} reshape(bf16[128,3072]{1,0:T(8,128)(2,1)} %fusion.1) | data formatting | bytes 1572864 | tf_op jit(solution)/shard_map/stack | solution.py:42
  14.5 0.0 copy-done.1
  14.5 2.1 %pad_maximum_fusion.2 = bf16[2,64,2,3072]{3,2,0,1:T(2,128)(2,1)S(1)} fusion(bf16[1,64,2,3072]{3,2,0,1:T(2,128)(2,1)S(1)} %bitcast.22, bf16[1,64,2,3072]{3,2,0,1:T(2,128)(2,1)S(1)} %bitcast.21), kind=kLoop, calls=%fused_computation.6 | loop fusion | flops 786432 | bytes 3145728 | tf_op jit(solution)/shard_map/stack | solution.py:42
  16.6 58.0 %all_to_all.18 = bf16[2,64,2,3072]{3,2,0,1:T(2,128)(2,1)S(1)} all-to-all(bf16[2,64,2,3072]{3,2,0,1:T(2,128)(2,1)S(1)} %pad_maximum_fusion.2), channel_id=1, replica_groups=mesh['tm'=8,'space'=4] {'tm'}, dimensions={1} | all-to-all | bytes 3145728 | tf_op jit(solution)/shard_map/all_to_all | solution.py:44
  74.6 1.7 %copy.16 = bf16[8,2,8,2,3072]{4,1,0,3,2:T(2,128)(2,1)S(1)} copy(bf16[8,2,8,2,3072]{4,3,1,2,0:T(2,128)(2,1)S(1)} %bitcast.20) | data formatting | bytes 3145728 | tf_op jit(solution)/shard_map/all_to_all | solution.py:44
  76.3 0.6 all_to_all.16
  76.9 0.5 fusion.14
  77.5 0.1 fusion.11
  77.6 18.4 %psum.7 = f32[8,2,15,15]{3,2,0,1:T(8,128)S(1)} all-reduce(f32[8,2,15,15]{3,2,0,1:T(8,128)S(1)} %fusion.6), channel_id=1, replica_groups=mesh['tm'=8,'space'=4] {'space'}, use_global_device_ids=true, to_apply=%region_0.1 | all-reduce | flops 3600 | bytes 28800 | tf_op jit(solution)/shard_map/psum | solution.py:68
  96.0 0.7 copy.17
  (3 shorter events, 0.1 us)
Async XLA Ops:
  0.0 5.0 %copy-start = (bf16[512,3072]{1,0:T(8,128)(2,1)S(1)}, bf16[512,3072]{1,0:T(8,128)(2,1)}, u32[]{:S(2)}) copy-start(bf16[512,3072]{1,0:T(8,128)(2,1)} %param.2) | copy-start | bytes 9437188
  0.0 4.2 %copy-start.2 = (s32[64]{0:T(128)S(1)}, s32[64]{0:T(128)}, u32[]{:S(2)}) copy-start(s32[64]{0:T(128)} %param.3) | copy-start | bytes 772
  2.8 6.5 %collective-permute-start = (bf16[256,3072]{1,0:T(8,128)(2,1)}, bf16[256,3072]{1,0:T(8,128)(2,1)}, u32[]{:S(2)}, u32[]{:S(2)}) collective-permute-start(bf16[256,3072]{1,0:T(8,128)(2,1)} %slice.21), channel_id=1, source_target_pairs={{4,0},{8,4},{12,8},{16,12},{20,16},{24,20},{28,24},{5,1},{9,5},{13... | collective-permute-start | bytes 4718600 | tf_op jit(solution)/shard_map/ppermute | solution.py:15
  12.3 2.2 %copy-start.1 = (bf16[1,64,2,3072]{3,2,1,0:T(2,128)(2,1)S(1)}, bf16[1,64,2,3072]{3,2,1,0:T(2,128)(2,1)}, u32[]{:S(2)}) copy-start(bf16[1,64,2,3072]{3,2,1,0:T(2,128)(2,1)} %stack.25) | copy-start | bytes 2359300
where the time goes:
time: 97 us; the launch traced here: 96.8 us
  blocking collectives  76.4 us (79%)
  local copies, waits for them, and re-layouts  11.2 us (12%)
  matrix products  4.92 us (5%)
  other arithmetic  2.86 us (3%)
  starting transfers between devices  1.28 us (1%)
    all_to_all x1, blocking collectives, local(): lax.all_to_all(owned, 'tm', split_axis=1, concat_axis=0, tiled=True)  58 us
    psum x1, blocking collectives, local(): return lax.psum(resident_gram_matrix, 'space')  18.4 us
    another operation x2, local copies, waits for them, and re-layouts, local(): owned = jnp.stack(pieces, axis=0).astype(jnp.bfloat16)  5.07 us
    dot_general x2, matrix products, local(): result = jnp.dot(table, segment, preferred_element_type=jnp.float32)  4.38 us
    slice x1, local copies, waits for them, and re-layouts, local(): leading = shifted(snapshots[:hop_len], 'tm', -1)  2.83 us
    all_to_all x2, local copies, waits for them, and re-layouts, local(): lax.all_to_all(owned, 'tm', split_axis=1, concat_axis=0, tiled=True)  2.33 us
    another operation x1, other arithmetic, local(): owned = jnp.stack(pieces, axis=0).astype(jnp.bfloat16)  2.07 us
  transfers between devices with their start and end apart: 1, of which 0 were waited for; matrix products, arithmetic and copies ran while one was open for 5% of the time, Pallas kernels for 0%

commit v1 on v0

v1 whole, which is shorter than its diff:
```python
import functools
import math

import jax
import jax.numpy as jnp
from jax import lax
from jax.experimental import pallas as pl
from jax.experimental.pallas import tpu as pltpu
from jax.sharding import PartitionSpec as P


NFFT = 512
HOP = NFFT // 2


ON_CHIP = pl.BlockSpec(memory_space=pltpu.VMEM)
IN_PLACE = pl.BlockSpec(memory_space=pltpu.HBM)


def bf16(*shape):
    return jax.ShapeDtypeStruct(shape, jnp.bfloat16)


def call(body, args, out_shape, in_specs=None, scratch=(), flops=0, moved=0, grant=24):
    return pl.pallas_call(
        body,
        in_specs=in_specs or [ON_CHIP] * len(args),
        out_specs=jax.tree.map(lambda _: ON_CHIP, out_shape),
        out_shape=out_shape,
        scratch_shapes=scratch,
        cost_estimate=pl.CostEstimate(flops=flops, bytes_accessed=moved, transcendentals=0),
        compiler_params=pltpu.CompilerParams(vmem_limit_bytes=grant << 20),
    )(*args)


def add(a, b):
    return (a.astype(jnp.float32) + b.astype(jnp.float32)).astype(jnp.bfloat16)


def cosine(phase):
    quarter = jnp.abs(phase - NFFT // 2) - NFFT // 4
    x = quarter.astype(jnp.float32) * (2.0 * math.pi / NFFT)
    square = x * x
    value = jnp.full_like(x, 1.0 / math.factorial(13))
    for order in (11, 9, 7, 5, 3, 1):
        value = value * square + (-1.0) ** (order // 2) / math.factorial(order)
    return value * x


def half_tables(freq_ref, chips, per_owner, chip, core):
    count = freq_ref.shape[1]
    row = lax.broadcasted_iota(jnp.int32, (2 * count, count), 0)
    lane = lax.broadcasted_iota(jnp.int32, (2 * count, count), 1)
    rows = 2 * per_owner
    away = (row // rows) % chips
    owner = 2 * (away ^ chip) + ((row // (rows * chips)) ^ core)
    picked = jnp.where(lane == owner * per_owner + row % per_owner, freq_ref[...], 0)
    freq = jnp.sum(picked.astype(jnp.float32), axis=1, keepdims=True).astype(jnp.int32)
    shape = (2 * count, HOP)
    part = (lax.broadcasted_iota(jnp.int32, shape, 0) // per_owner) % 2
    shift = lax.broadcasted_iota(jnp.int32, shape, 1)
    wave = cosine((freq * shift + part * (NFFT // 4)) & (NFFT - 1))
    taper = 0.5 * cosine(lax.broadcasted_iota(jnp.int32, (8, HOP), 1))[:1]
    sign = (1 - 2 * (freq & 1)).astype(jnp.float32)
    early = ((0.5 - taper) * wave).astype(jnp.bfloat16)
    late = ((0.5 + taper) * (wave * sign)).astype(jnp.bfloat16)
    return early, late


def transform_body(chips, rows, freq_ref, snap_ref, own_ref, other_ref, *refs):
    far_refs, (stage, sems) = refs[:-2], refs[-2:]
    device = lax.axis_index("tm")
    points = snap_ref.shape[1]
    pieces = sems.shape[0]
    block = points // pieces
    copies = [
        pltpu.make_async_copy(
            snap_ref.at[:, pl.ds(i * block, block)], stage.at[:, pl.ds(i * block, block)], sems.at[i]
        )
        for i in range(pieces)
    ]
    for copy in copies:
        copy.start()
    early, late = half_tables(freq_ref, chips, rows // 2, device // 2, device % 2)
    table = jnp.concatenate([early, late], axis=0)
    half = early.shape[0]
    for i, copy in enumerate(copies):
        copy.wait()
        columns = pl.ds(i * block, block)
        first = jnp.dot(table, stage[:HOP, columns], preferred_element_type=jnp.float32)
        second = jnp.dot(table, stage[HOP:, columns], preferred_element_type=jnp.float32)
        units = (first[:half] + second[half:], first[half:], second[:half])
        for u, unit in enumerate(units):
            unit = unit.astype(jnp.bfloat16)
            for s in range(chips):
                value = unit[s * rows : (s + 1) * rows]
                if u == 0 and s >= 2:
                    far_refs[s - 2][:, columns] = value
                else:
                    own_ref[u, s, :, columns] = value
                other_ref[u, s, :, columns] = unit[half // 2 + s * rows : half // 2 + (s + 1) * rows]


def spread_body(chips, own_ref, got_ref, halo_ref, near_ref, loc_ref, keep_ref, *main_refs):
    device = lax.axis_index("tm")
    chip, core = device // 2, device % 2

    def write(low, high):
        for s, ref in ((0, loc_ref), (1, near_ref)):
            ref[0] = low[0, s]
            ref[1] = add(low[2, s], high[1, s])
            ref[2] = high[0, s]
            ref[3] = low[1, s]
            ref[4] = high[2, s]
        for s in range(2, chips):
            main_refs[s - 2][0] = add(low[2, s], high[1, s])
            main_refs[s - 2][1] = got_ref[0, s]

        def outer(toward, away):
            for s in range(2, chips):
                halo_ref[s - 2] = toward(s ^ 1)
                keep_ref[0, s - 2] = toward(s)
                keep_ref[1, s - 2] = away(s)

        @pl.when(chip % 2 == 0)
        def _():
            outer(lambda s: high[2, s], lambda s: low[1, s])

        @pl.when(chip % 2 == 1)
        def _():
            outer(lambda s: low[1, s], lambda s: high[2, s])

    @pl.when(core == 0)
    def _():
        write(own_ref, got_ref)

    @pl.when(core == 1)
    def _():
        write(got_ref, own_ref)


def merge_body(chips, keep_ref, halo_ref, *out_refs):
    for s in range(2, chips):
        out_refs[s - 2][0] = add(keep_ref[0, s - 2], halo_ref[s - 2])
        out_refs[s - 2][1] = keep_ref[1, s - 2]


def gram_body(chips, scale, loc_ref, near_ref, *refs):
    count = chips - 2
    owns, mains, extras = refs[:count], refs[count : 2 * count], refs[2 * count : 3 * count]
    thirds = refs[3 * count : -2]
    out_ref, data = refs[-2:]
    slots, rows, points = data.shape
    device = lax.axis_index("tm")
    chip, core = device // 2, device % 2

    def accumulate(slot, value):
        slot = lax.rem(slot + slots, slots)
        data[slot] = add(data[slot], value)

    for y in range(chips):
        data[4 * y + 3] = jnp.zeros((rows, points), jnp.bfloat16)
    for y, ref in ((chip, loc_ref), (chip ^ 1, near_ref)):
        for j in range(3):
            data[4 * y + j] = ref[j]
        accumulate(4 * y - 1, ref[3])
        accumulate(4 * y + 3, ref[4])
    for s in range(2, chips):
        y = chip ^ s
        odd = y % 2 == 1
        away = jnp.where(odd, 4 * y + 3, 4 * y - 1)
        data[4 * y + 2 * core] = owns[s - 2][...]
        data[4 * y + 1] = mains[s - 2][0]
        data[4 * y + 2 - 2 * core] = mains[s - 2][1]

        @pl.when(odd == (chip > y))
        def _():
            accumulate(4 * (y - y % 2) + 3, extras[s - 2][0])
            accumulate(away, extras[s - 2][1])

        if thirds:

            @pl.when(odd != (chip > y))
            def _():
                accumulate(away, thirds[s - 2][0])

    whole = data[...].reshape(slots * rows, points)
    total = lax.dot_general(whole, whole, (((1,), (1,)), ((), ())), preferred_element_type=jnp.float32)
    per = rows // 2
    size = slots * rows
    row = lax.broadcasted_iota(jnp.int32, (size, size), 0)
    lane = lax.broadcasted_iota(jnp.int32, (size, size), 1)
    picked = jnp.where(row % per == lane % per, total, 0.0).reshape(slots, 2, per, size).sum(axis=2)
    real, imag = picked[:, 0], picked[:, 1]
    second = (lax.broadcasted_iota(jnp.int32, (slots, size), 1) // per) % 2 == 1
    diagonal = real + pltpu.roll(imag, size - per, 1)
    crossed = pltpu.roll(imag, per, 1) - real
    out_ref[...] = jnp.where(second, crossed, diagonal) * scale


def reduce_space(value):
    count = lax.axis_size("space")
    stride = 1
    while stride < count:
        step = 4 if stride * 4 <= count else 2
        parts = [value] + [
            lax.ppermute(value, "space", [(i, i ^ (stride * s)) for i in range(count)]) for s in range(1, step)
        ]
        while len(parts) > 1:
            parts = [a + b for a, b in zip(parts[::2], parts[1::2])]
        value = parts[0]
        stride *= step
    return value


def local(snapshots, freq_ids):
    devices = lax.axis_size("tm")
    chips = devices // 2
    far = range(2, chips)
    count = chips - 2
    blocks = 2 * devices - 1
    slots = 2 * devices
    points = snapshots.shape[1]
    per_owner = freq_ids.shape[0] // devices
    rows = 2 * per_owner

    def across(value, s, keep=lambda y: True):
        route = [(2 * y + c, 2 * (y ^ s) + c) for y in range(chips) for c in range(2) if keep(y)]
        return lax.ppermute(value, "tm", route)

    def outward(s):
        return lambda y: (y % 2 == 1) == ((y ^ s) > y)

    def third(s):
        return lambda y: (y % 2 == 1) != ((y ^ s) > y) and y not in (0, chips - 1)

    size = 4 * freq_ids.shape[0] * points
    pieces = 6 if points % 768 == 0 else 1
    own, other, *owns = call(
        functools.partial(transform_body, chips, rows),
        (freq_ids.reshape(1, -1), snapshots),
        [bf16(3, chips, rows, points)] * 2 + [bf16(rows, points)] * count,
        [ON_CHIP, IN_PLACE],
        [pltpu.VMEM((NFFT, points), jnp.bfloat16), pltpu.SemaphoreType.DMA((pieces,))],
        flops=4 * size * HOP,
        moved=5 * size,
        grant=24,
    )
    got = lax.ppermute(other, "tm", [(i, i ^ 1) for i in range(devices)])
    owns = [across(owns[s - 2], s) for s in far]
    halo, near, loc, keep, *mains = call(
        functools.partial(spread_body, chips),
        (own, got),
        [
            bf16(count, rows, points),
            bf16(5, rows, points),
            bf16(5, rows, points),
            bf16(2, count, rows, points),
            *([bf16(2, rows, points)] * count),
        ],
        moved=5 * size,
    )
    halo = across(halo, 1, lambda y: chips > 4 or y in (0, chips - 1))
    near = across(near, 1)
    mains = [across(mains[s - 2], s) for s in far]
    extras = call(
        functools.partial(merge_body, chips),
        (keep, halo),
        [bf16(2, rows, points)] * count,
        moved=2 * size,
    )
    thirds = []
    if chips > 4:
        thirds = [across(keep[1:, s - 2], s, third(s)) for s in far]
    extras = [across(extras[s - 2], s, outward(s)) for s in far]
    scale = 1.0 / (NFFT * points * lax.axis_size("space"))
    total = slots * rows
    reduced = call(
        functools.partial(gram_body, chips, scale),
        (loc, near, *owns, *mains, *extras, *thirds),
        jax.ShapeDtypeStruct((slots, total), jnp.float32),
        None,
        [pltpu.VMEM((slots, rows, points), jnp.bfloat16)],
        flops=2 * total * total * points,
        moved=2 * total * points,
    )
    reduced = reduce_space(reduced)
    parts = reduced.reshape(slots, slots, 2, per_owner)[:blocks, :blocks]
    return jnp.transpose(parts, (3, 2, 0, 1))


def solution(mesh):
    return jax.shard_map(
        local,
        mesh=mesh,
        in_specs=(P("tm", "space"), P()),
        out_specs=P("tm", None, None, None),
        check_vma=False,
    )
```

time: 97 us -> 60.9 us (0.63)
  the two profiles are of different devices: /device:TPU:0 before, /device:TPU:8 now
where the time goes in v1:
time: 60.9 us; the launch traced here: 60.7 us
  waiting for transfers between devices  35.7 us (59%)
  starting transfers between devices  17.7 us (29%)
  Pallas kernels  3.76 us (6%)
  local copies, waits for them, and re-layouts  3.51 us (6%)
    ppermute x8, waiting for transfers between devices, across(): return lax.ppermute(value, 'tm', route)  29.6 us
    ppermute x8, starting transfers between devices, across(): return lax.ppermute(value, 'tm', route)  14.1 us
    pallas_call x4, Pallas kernels, call(): pl.pallas_call(body, in_specs=in_specs or [ON_CHIP] * len(args), out_spec...  3.76 us
    ppermute x3, starting transfers between devices, reduce_space(): lax.ppermute(value, 'space', [(i, i ^ stride * s) for i in range(count)])  3.52 us
    ppermute x3, waiting for transfers between devices, reduce_space(): lax.ppermute(value, 'space', [(i, i ^ stride * s) for i in range(count)])  3.2 us
    ppermute x1, waiting for transfers between devices, local(): got = lax.ppermute(other, 'tm', [(i, i ^ 1) for i in range(devices)])  2.83 us
    unnamed x4, local copies, waits for them, and re-layouts  2.54 us
  transfers between devices with their start and end apart: 12, of which 10 were waited for; matrix products, arithmetic and copies ran while one was open for 0% of the time, Pallas kernels for 0%

profile of v1, /device:TPU:8, one launch (start us, length us, event | category | flops | bytes accessed | tf_op | source)
XLA Modules:
  0.0 60.7 jit_solution(5138202663806208528)
XLA Ops:
  0.0 1.9 %copy-done = bf16[512,3072]{1,0:T(8,128)(2,1)S(1)} copy-done((bf16[512,3072]{1,0:T(8,128)(2,1)S(1)}, bf16[512,3072]{1,0:T(8,128)(2,1)}, u32[]{:S(2)}) %copy-start) | copy-done | bytes 3145752
  1.9 0.7 %copy-done.1 = s32[64]{0:T(128)S(1)} copy-done((s32[64]{0:T(128)S(1)}, s32[64]{0:T(128)}, u32[]{:S(2)}) %copy-start.1) | copy-done | bytes 280
  2.5 2.5 %shard_map.28 = (bf16[3,4,16,3072]{3,2,1,0:T(8,128)(2,1)S(1)}, bf16[3,4,16,3072]{3,2,1,0:T(8,128)(2,1)S(1)}, bf16[16,3072]{1,0:T(8,128)(2,1)S(1)}, bf16[16,3072]{1,0:T(8,128)(2,1)S(1)}) custom-call(s32[1,64]{1,0:T(1,128)S(1)} %bitcast.4, bf16[512,3072]{1,0:T(8,128)(2,1)S(1)} %copy-done), custom_call_target="tpu_custom_call" | custom-call | flops 805306368 | bytes 3932160 | tf_op jit(solution)/shard_map/pallas_call | solution.py:25
  5.2 2.8 %collective-permute-done.got_ref = bf16[3,4,16,3072]{3,2,1,0:T(8,128)(2,1)S(1)} collective-permute-done((bf16[3,4,16,3072]{3,2,1,0:T(8,128)(2,1)S(1)}, bf16[3,4,16,3072]{3,2,1,0:T(8,128)(2,1)S(1)}, u32[]{:S(2)}, u32[]{:S(2)}) %collective-permute-start) | collective-permute-done | bytes 1179680 | tf_op jit(solution)/shard_map/ppermute | solution.py:249
  8.2 1.3 %collective-permute-start.6 = (bf16[2,16,3072]{2,1,0:T(8,128)(2,1)S(1)}, bf16[2,16,3072]{2,1,0:T(8,128)(2,1)S(1)}, u32[]{:S(2)}, u32[]{:S(2)}) collective-permute-start(bf16[2,16,3072]{2,1,0:T(8,128)(2,1)S(1)} %get-tuple-element.26), channel_id=1, source_target_pairs={{0,8},{4,12},{24,16},{28,20},{1,9},{5,13},{25,17},{29,21},{2,10},{... | collective-permute-start | bytes 589832 | tf_op jit(solution)/shard_map/ppermute | solution.py:229
  9.5 5.3 %collective-permute-start.2 = (bf16[16,3072]{1,0:T(8,128)(2,1)S(1)}, bf16[16,3072]{1,0:T(8,128)(2,1)S(1)}, u32[]{:S(2)}, u32[]{:S(2)}) collective-permute-start(bf16[16,3072]{1,0:T(8,128)(2,1)S(1)} %get-tuple-element.21), channel_id=1, source_target_pairs={{0,16},{4,20},{8,24},{12,28},{16,0},{20,4},{24,8},{28,12},{1,17},{... | collective-permute-start | bytes 294920 | tf_op jit(solution)/shard_map/ppermute | solution.py:229
  14.8 1.7 %collective-permute-start.4 = (bf16[2,16,3072]{2,1,0:T(8,128)(2,1)S(1)}, bf16[2,16,3072]{2,1,0:T(8,128)(2,1)S(1)}, u32[]{:S(2)}, u32[]{:S(2)}) collective-permute-start(bf16[2,16,3072]{2,1,0:T(8,128)(2,1)S(1)} %get-tuple-element.23), channel_id=1, source_target_pairs={{0,16},{4,20},{8,24},{12,28},{16,0},{20,4},{24,8},{28,12},{1,17},{... | collective-permute-start | bytes 589832 | tf_op jit(solution)/shard_map/ppermute | solution.py:229
  16.6 10.0 %collective-permute-done.6.halo_ref = bf16[2,16,3072]{2,1,0:T(8,128)(2,1)S(1)} collective-permute-done((bf16[2,16,3072]{2,1,0:T(8,128)(2,1)S(1)}, bf16[2,16,3072]{2,1,0:T(8,128)(2,1)S(1)}, u32[]{:S(2)}, u32[]{:S(2)}) %collective-permute-start.6) | collective-permute-done | bytes 196640 | tf_op jit(solution)/shard_map/ppermute | solution.py:229
  26.5 1.6 %collective-permute-start.5 = (bf16[2,16,3072]{2,1,0:T(8,128)(2,1)S(1)}, bf16[2,16,3072]{2,1,0:T(8,128)(2,1)S(1)}, u32[]{:S(2)}, u32[]{:S(2)}) collective-permute-start(bf16[2,16,3072]{2,1,0:T(8,128)(2,1)S(1)} %get-tuple-element.24), channel_id=1, source_target_pairs={{0,24},{4,28},{8,16},{12,20},{16,8},{20,12},{24,0},{28,4},{1,25},{... | collective-permute-start | bytes 589832 | tf_op jit(solution)/shard_map/ppermute | solution.py:229
  28.2 1.6 %collective-permute-done.2.refs_0_ = bf16[16,3072]{1,0:T(8,128)(2,1)S(1)} collective-permute-done((bf16[16,3072]{1,0:T(8,128)(2,1)S(1)}, bf16[16,3072]{1,0:T(8,128)(2,1)S(1)}, u32[]{:S(2)}, u32[]{:S(2)}) %collective-permute-start.2) | collective-permute-done | bytes 98336 | tf_op jit(solution)/shard_map/ppermute | solution.py:229
  29.8 1.4 %collective-permute-start.7 = (bf16[2,16,3072]{2,1,0:T(8,128)(2,1)S(1)}, bf16[2,16,3072]{2,1,0:T(8,128)(2,1)S(1)}, u32[]{:S(2)}, u32[]{:S(2)}) collective-permute-start(bf16[2,16,3072]{2,1,0:T(8,128)(2,1)S(1)} %get-tuple-element.27), channel_id=1, source_target_pairs={{8,24},{12,28},{16,0},{20,4},{9,25},{13,29},{17,1},{21,5},{10,26},... | collective-permute-start | bytes 589832 | tf_op jit(solution)/shard_map/ppermute | solution.py:229
  31.2 2.8 %collective-permute-start.8 = (bf16[2,16,3072]{2,1,0:T(8,128)(2,1)S(1)}, bf16[2,16,3072]{2,1,0:T(8,128)(2,1)S(1)}, u32[]{:S(2)}, u32[]{:S(2)}) collective-permute-start(bf16[2,16,3072]{2,1,0:T(8,128)(2,1)S(1)} %get-tuple-element.28), channel_id=1, source_target_pairs={{8,16},{12,20},{16,8},{20,12},{9,17},{13,21},{17,9},{21,13},{10,18... | collective-permute-start | bytes 589832 | tf_op jit(solution)/shard_map/ppermute | solution.py:229
  33.9 2.1 %collective-permute-done.4.refs_2_ = bf16[2,16,3072]{2,1,0:T(8,128)(2,1)S(1)} collective-permute-done((bf16[2,16,3072]{2,1,0:T(8,128)(2,1)S(1)}, bf16[2,16,3072]{2,1,0:T(8,128)(2,1)S(1)}, u32[]{:S(2)}, u32[]{:S(2)}) %collective-permute-start.4) | collective-permute-done | bytes 196640 | tf_op jit(solution)/shard_map/ppermute | solution.py:229
  36.1 7.6 %collective-permute-done.5.refs_3_ = bf16[2,16,3072]{2,1,0:T(8,128)(2,1)S(1)} collective-permute-done((bf16[2,16,3072]{2,1,0:T(8,128)(2,1)S(1)}, bf16[2,16,3072]{2,1,0:T(8,128)(2,1)S(1)}, u32[]{:S(2)}, u32[]{:S(2)}) %collective-permute-start.5) | collective-permute-done | bytes 196640 | tf_op jit(solution)/shard_map/ppermute | solution.py:229
  43.7 2.2 %collective-permute-done.7.refs_4_ = bf16[2,16,3072]{2,1,0:T(8,128)(2,1)S(1)} collective-permute-done((bf16[2,16,3072]{2,1,0:T(8,128)(2,1)S(1)}, bf16[2,16,3072]{2,1,0:T(8,128)(2,1)S(1)}, u32[]{:S(2)}, u32[]{:S(2)}) %collective-permute-start.7) | collective-permute-done | bytes 196640 | tf_op jit(solution)/shard_map/ppermute | solution.py:229
  45.9 6.1 %collective-permute-done.8.refs_5_ = bf16[2,16,3072]{2,1,0:T(8,128)(2,1)S(1)} collective-permute-done((bf16[2,16,3072]{2,1,0:T(8,128)(2,1)S(1)}, bf16[2,16,3072]{2,1,0:T(8,128)(2,1)S(1)}, u32[]{:S(2)}, u32[]{:S(2)}) %collective-permute-start.8) | collective-permute-done | bytes 196640 | tf_op jit(solution)/shard_map/ppermute | solution.py:229
  52.0 1.0 %shard_map.31 = f32[16,256]{1,0:T(8,128)S(1)} custom-call(bf16[5,16,3072]{2,1,0:T(8,128)(2,1)S(1)} %get-tuple-element.19.loc_ref, bf16[5,16,3072]{2,1,0:T(8,128)(2,1)S(1)} %collective-permute-done.1.near_ref, bf16[16,3072]{1,0:T(8,128)(2,1)S(1)} %collective-permute-done.2.refs_0_, bf16[16,3072]{1,0:T(8,128)(2,1)S(1)} %collective-permute-done.3.refs_1_, ...), custom_call_target="tpu_custom_call" | custom-call | flops 402653184 | bytes 1572864 | tf_op jit(solution)/shard_map/pallas_call | solution.py:25
  53.0 2.5 %collective-permute-start.11 = (f32[16,256]{1,0:T(8,128)S(1)}, f32[16,256]{1,0:T(8,128)S(1)}, u32[]{:S(2)}, u32[]{:S(2)}) collective-permute-start(f32[16,256]{1,0:T(8,128)S(1)} %shard_map.31), channel_id=1, source_target_pairs={{0,3},{1,2},{2,1},{3,0},{4,7},{5,6},{6,5},{7,4},{8,11},{9,10},{10,... | collective-permute-start | bytes 49160 | tf_op jit(solution)/shard_map/ppermute | solution.py:207
  55.5 0.5 collective-permute-start.10
  56.0 0.5 collective-permute-start.9
  56.6 1.1 %collective-permute-done.11 = f32[16,256]{1,0:T(8,128)S(1)} collective-permute-done((f32[16,256]{1,0:T(8,128)S(1)}, f32[16,256]{1,0:T(8,128)S(1)}, u32[]{:S(2)}, u32[]{:S(2)}) %collective-permute-start.11) | collective-permute-done | bytes 16416 | tf_op jit(solution)/shard_map/ppermute | solution.py:207
  57.7 1.5 %collective-permute-done.10 = f32[16,256]{1,0:T(8,128)S(1)} collective-permute-done((f32[16,256]{1,0:T(8,128)S(1)}, f32[16,256]{1,0:T(8,128)S(1)}, u32[]{:S(2)}, u32[]{:S(2)}) %collective-permute-start.10) | collective-permute-done | bytes 16416 | tf_op jit(solution)/shard_map/ppermute | solution.py:207
  59.3 0.5 collective-permute-done.9
  59.9 0.9 %copy.5 = f32[8,2,15,15]{3,1,2,0:T(2,128)} copy(f32[8,2,15,15]{2,0,1,3:T(8,128)S(1)} %slice_bitcast_fusion) | data formatting | bytes 28800 | tf_op jit(solution)/shard_map/transpose | solution.py:289
  (12 shorter events, 0.5 us)
Async XLA Ops:
  0.0 1.9 %copy-start = (bf16[512,3072]{1,0:T(8,128)(2,1)S(1)}, bf16[512,3072]{1,0:T(8,128)(2,1)}, u32[]{:S(2)}) copy-start(bf16[512,3072]{1,0:T(8,128)(2,1)} %snap_ref.1) | copy-start | bytes 9437188
  1.9 0.7 %copy-start.1 = (s32[64]{0:T(128)S(1)}, s32[64]{0:T(128)}, u32[]{:S(2)}) copy-start(s32[64]{0:T(128)} %param.3) | copy-start | bytes 772
  5.1 2.9 %collective-permute-start = (bf16[3,4,16,3072]{3,2,1,0:T(8,128)(2,1)S(1)}, bf16[3,4,16,3072]{3,2,1,0:T(8,128)(2,1)S(1)}, u32[]{:S(2)}, u32[]{:S(2)}) collective-permute-start(bf16[3,4,16,3072]{3,2,1,0:T(8,128)(2,1)S(1)} %get-tuple-element.18), channel_id=1, source_target_pairs={{0,4},{4,0},{8,12},{12,8},{16,20},{20,16},{24,28},{28,24},{1,5},{5... | collective-permute-start | bytes 3538952 | tf_op jit(solution)/shard_map/ppermute | solution.py:249
  8.2 43.8 %collective-permute-start.1 = (bf16[5,16,3072]{2,1,0:T(8,128)(2,1)S(1)}, bf16[5,16,3072]{2,1,0:T(8,128)(2,1)S(1)}, u32[]{:S(2)}, u32[]{:S(2)}) collective-permute-start(bf16[5,16,3072]{2,1,0:T(8,128)(2,1)S(1)} %get-tuple-element.20), channel_id=1, source_target_pairs={{0,8},{4,12},{8,0},{12,4},{16,24},{20,28},{24,16},{28,20},{1,9},{5... | collective-permute-start | bytes 1474568 | tf_op jit(solution)/shard_map/ppermute | solution.py:229
  8.2 18.3 %collective-permute-start.6 = (bf16[2,16,3072]{2,1,0:T(8,128)(2,1)S(1)}, bf16[2,16,3072]{2,1,0:T(8,128)(2,1)S(1)}, u32[]{:S(2)}, u32[]{:S(2)}) collective-permute-start(bf16[2,16,3072]{2,1,0:T(8,128)(2,1)S(1)} %get-tuple-element.26), channel_id=1, source_target_pairs={{0,8},{4,12},{24,16},{28,20},{1,9},{5,13},{25,17},{29,21},{2,10},{... | collective-permute-start | bytes 589832 | tf_op jit(solution)/shard_map/ppermute | solution.py:229
  9.5 20.2 %collective-permute-start.2 = (bf16[16,3072]{1,0:T(8,128)(2,1)S(1)}, bf16[16,3072]{1,0:T(8,128)(2,1)S(1)}, u32[]{:S(2)}, u32[]{:S(2)}) collective-permute-start(bf16[16,3072]{1,0:T(8,128)(2,1)S(1)} %get-tuple-element.21), channel_id=1, source_target_pairs={{0,16},{4,20},{8,24},{12,28},{16,0},{20,4},{24,8},{28,12},{1,17},{... | collective-permute-start | bytes 294920 | tf_op jit(solution)/shard_map/ppermute | solution.py:229
  14.8 16.3 %collective-permute-start.3 = (bf16[16,3072]{1,0:T(8,128)(2,1)S(1)}, bf16[16,3072]{1,0:T(8,128)(2,1)S(1)}, u32[]{:S(2)}, u32[]{:S(2)}) collective-permute-start(bf16[16,3072]{1,0:T(8,128)(2,1)S(1)} %get-tuple-element.22), channel_id=1, source_target_pairs={{0,24},{4,28},{8,16},{12,20},{16,8},{20,12},{24,0},{28,4},{1,25},{... | collective-permute-start | bytes 294920 | tf_op jit(solution)/shard_map/ppermute | solution.py:229
  14.8 21.2 %collective-permute-start.4 = (bf16[2,16,3072]{2,1,0:T(8,128)(2,1)S(1)}, bf16[2,16,3072]{2,1,0:T(8,128)(2,1)S(1)}, u32[]{:S(2)}, u32[]{:S(2)}) collective-permute-start(bf16[2,16,3072]{2,1,0:T(8,128)(2,1)S(1)} %get-tuple-element.23), channel_id=1, source_target_pairs={{0,16},{4,20},{8,24},{12,28},{16,0},{20,4},{24,8},{28,12},{1,17},{... | collective-permute-start | bytes 589832 | tf_op jit(solution)/shard_map/ppermute | solution.py:229
  26.5 17.1 %collective-permute-start.5 = (bf16[2,16,3072]{2,1,0:T(8,128)(2,1)S(1)}, bf16[2,16,3072]{2,1,0:T(8,128)(2,1)S(1)}, u32[]{:S(2)}, u32[]{:S(2)}) collective-permute-start(bf16[2,16,3072]{2,1,0:T(8,128)(2,1)S(1)} %get-tuple-element.24), channel_id=1, source_target_pairs={{0,24},{4,28},{8,16},{12,20},{16,8},{20,12},{24,0},{28,4},{1,25},{... | collective-permute-start | bytes 589832 | tf_op jit(solution)/shard_map/ppermute | solution.py:229
  29.8 16.1 %collective-permute-start.7 = (bf16[2,16,3072]{2,1,0:T(8,128)(2,1)S(1)}, bf16[2,16,3072]{2,1,0:T(8,128)(2,1)S(1)}, u32[]{:S(2)}, u32[]{:S(2)}) collective-permute-start(bf16[2,16,3072]{2,1,0:T(8,128)(2,1)S(1)} %get-tuple-element.27), channel_id=1, source_target_pairs={{8,24},{12,28},{16,0},{20,4},{9,25},{13,29},{17,1},{21,5},{10,26},... | collective-permute-start | bytes 589832 | tf_op jit(solution)/shard_map/ppermute | solution.py:229
  31.2 20.8 %collective-permute-start.8 = (bf16[2,16,3072]{2,1,0:T(8,128)(2,1)S(1)}, bf16[2,16,3072]{2,1,0:T(8,128)(2,1)S(1)}, u32[]{:S(2)}, u32[]{:S(2)}) collective-permute-start(bf16[2,16,3072]{2,1,0:T(8,128)(2,1)S(1)} %get-tuple-element.28), channel_id=1, source_target_pairs={{8,16},{12,20},{16,8},{20,12},{9,17},{13,21},{17,9},{21,13},{10,18... | collective-permute-start | bytes 589832 | tf_op jit(solution)/shard_map/ppermute | solution.py:229
  53.0 4.7 %collective-permute-start.11 = (f32[16,256]{1,0:T(8,128)S(1)}, f32[16,256]{1,0:T(8,128)S(1)}, u32[]{:S(2)}, u32[]{:S(2)}) collective-permute-start(f32[16,256]{1,0:T(8,128)S(1)} %shard_map.31), channel_id=1, source_target_pairs={{0,3},{1,2},{2,1},{3,0},{4,7},{5,6},{6,5},{7,4},{8,11},{9,10},{10,... | collective-permute-start | bytes 49160 | tf_op jit(solution)/shard_map/ppermute | solution.py:207
  55.5 3.7 %collective-permute-start.10 = (f32[16,256]{1,0:T(8,128)S(1)}, f32[16,256]{1,0:T(8,128)S(1)}, u32[]{:S(2)}, u32[]{:S(2)}) collective-permute-start(f32[16,256]{1,0:T(8,128)S(1)} %shard_map.31), channel_id=1, source_target_pairs={{0,2},{1,3},{2,0},{3,1},{4,6},{5,7},{6,4},{7,5},{8,10},{9,11},{10,... | collective-permute-start | bytes 49160 | tf_op jit(solution)/shard_map/ppermute | solution.py:207
  56.0 3.7 %collective-permute-start.9 = (f32[16,256]{1,0:T(8,128)S(1)}, f32[16,256]{1,0:T(8,128)S(1)}, u32[]{:S(2)}, u32[]{:S(2)}) collective-permute-start(f32[16,256]{1,0:T(8,128)S(1)} %shard_map.31), channel_id=1, source_target_pairs={{0,1},{1,0},{2,3},{3,2},{4,5},{5,4},{6,7},{7,6},{8,9},{9,8},{10,11... | collective-permute-start | bytes 49160 | tf_op jit(solution)/shard_map/ppermute | solution.py:207
